TPU v7x, 32 devices: a whole 2x2x4 slice. The times are simulated.
32 devices in a mesh: groups: 2 (over x), dp: 8 (over z, y), mp: 2 (over core).
Axes of the slice: x: 2, y: 2, z: 4, core: 2. Of those that a mesh axis runs over, the one named last changes fastest.
Arguments:
- residual: bfloat16 [48, 128, 8192], P(('groups', 'dp'), None, 'mp'), parts along dimension 0
- lengths: int32 [48], P(('groups', 'dp')), parts along dimension 0, may hold values from 32 to 128
- labels: int32 [48], P(('groups', 'dp')), parts along dimension 0, may hold values from 0 to 1, as said below
- earlier_means: float32 [16, 79, 2, 8192], P(('groups', 'dp'), None, None, 'mp'), parts along dimension 0
- chosen: int32 [2], P('groups'), parts along dimension 0, may hold values from 0 to 79
- norm_gain: float32 [8192], P('mp'), may hold values from 0.1 to 1.9
- key_weight: bfloat16 [2, 4096, 1024], P('mp', 'dp'), may hold values from -0.0625 to 0.0625
- value_weight: bfloat16 [2, 4096, 1024], P('mp', 'dp'), may hold values from -0.0625 to 0.0625
- out_proj: bfloat16 [2, 8192, 8192], P('groups', 'mp', 'dp'), parts along dimension 0
Outputs:
- directions: float32 [160, 8192], P('groups', 'mp'), parts along dimension 0
- key_cache: bfloat16 [48, 128, 1024], P(('groups', 'dp'), None, 'mp'), parts along dimension 0
- value_cache: bfloat16 [48, 128, 1024], P(('groups', 'dp'), None, 'mp'), parts along dimension 0
- ortho_proj: bfloat16 [2, 8192, 8192], P('groups', 'mp', 'dp'), parts along dimension 0
There are 2 independent parts, one for each index of `groups`. A program takes and returns all parts, laid end to end along the dimension named above; an argument that names none is the same for every part. Nothing has to cross between parts.
Inputs may be any that keep to these rules, and one draw needn't show every extreme that they name: Every slab of 3 consecutive prompts holds both labels.
All inputs are finite; a program needn't handle non-finite values.
Results may differ from a plain program's by a relative error of at most 0.0051.
Values may be sent and summed in bfloat16 or wider, within the bound.
A program may use at most 384 MiB of HBM per device.

v0:
```python
import math
import jax
import jax.numpy as jnp
from jax import lax
from jax.sharding import PartitionSpec as P


def joined(value, axis, join):
    pieces = jax.tree.map(lambda part: lax.all_gather(part, axis), value)
    head = jax.tree.map(lambda part: part[0], pieces)
    tail = jax.tree.map(lambda part: part[1:], pieces)
    total, _ = lax.scan(lambda total, share: (join(total, share), None), head, tail)
    return total


def shards(
    residual, lengths, labels, earlier_means, chosen, norm_gain, key_weight, value_weight, out_proj
):
    highest = lax.Precision.HIGHEST
    prompts, length, half_width = residual.shape
    model_width = half_width * lax.axis_size("mp")
    positions = jnp.arange(length, dtype=jnp.int32)
    valid_mask = (positions[None, :] < lengths[:, None]).astype(jnp.bfloat16)
    masked_sums = jnp.einsum("pt,ptd->pd", valid_mask, residual, preferred_element_type=jnp.float32)
    prompt_mean = masked_sums / lengths.astype(jnp.float32)[:, None]
    onehot = (labels[:, None] == jnp.arange(2, dtype=jnp.int32)[None, :]).astype(jnp.float32)
    counts = jnp.sum(onehot, axis=0)
    current = jnp.dot(onehot.T, prompt_mean, precision=highest) / counts[:, None]
    layer_means = jnp.concatenate([earlier_means[0], current[None]], axis=0)

    def combine(left_pair, right_pair):
        joint_count = left_pair[0] + right_pair[0]
        blended = (
            left_pair[0][None, :, None] * left_pair[1]
            + right_pair[0][None, :, None] * right_pair[1]
        )
        return (joint_count, blended / joint_count[None, :, None])

    merged_counts, merged = joined((counts, layer_means), "dp", combine)
    difference = merged[:, 1] - merged[:, 0]
    square_sums = lax.psum(jnp.sum(difference * difference, axis=1), "mp")
    mean_dir = square_sums / model_width
    inverse_rms = lax.rsqrt(mean_dir + 1e-06)
    directions = difference * inverse_rms[:, None]
    chosen_layer = chosen[0]
    refusal_dir = lax.dynamic_index_in_dim(directions, chosen_layer, 0, keepdims=False) / math.sqrt(
        model_width
    )
    token_rows = residual.reshape(prompts * length, half_width)
    row_values = token_rows.astype(jnp.float32)
    projection_local = jnp.dot(row_values, refusal_dir, precision=highest)
    column_local = jnp.einsum(
        "r,ori->oi", refusal_dir, out_proj.astype(jnp.float32), precision=highest
    )
    projection, column_proj = lax.psum((projection_local, column_local), "mp")
    ablated = row_values - projection[:, None] * refusal_dir[None, :]
    mean_square = lax.psum(jnp.sum(ablated * ablated, axis=1), "mp") / model_width
    normed = (ablated * lax.rsqrt(mean_square + 1e-05)[:, None] * norm_gain[None, :]).astype(
        jnp.bfloat16
    )
    key_sum = jnp.dot(
        normed,
        lax.all_gather(key_weight, "dp", axis=1, tiled=True)[0],
        preferred_element_type=jnp.float32,
    )
    value_sum = jnp.dot(
        normed,
        lax.all_gather(value_weight, "dp", axis=1, tiled=True)[0],
        preferred_element_type=jnp.float32,
    )
    key_sums, value_sums = (
        lax.psum_scatter(key_sum, "mp", scatter_dimension=1, tiled=True),
        lax.psum_scatter(value_sum, "mp", scatter_dimension=1, tiled=True),
    )
    key_cache = key_sums.astype(jnp.bfloat16).reshape(prompts, length, key_sums.shape[1])
    value_cache = value_sums.astype(jnp.bfloat16).reshape(prompts, length, value_sums.shape[1])
    ortho_proj = (
        out_proj.astype(jnp.float32) - refusal_dir[None, :, None] * column_proj[:, None, :]
    ).astype(jnp.bfloat16)
    return (directions, key_cache, value_cache, ortho_proj)


def solution(mesh):
    return jax.shard_map(
        shards,
        mesh=mesh,
        in_specs=(
            P(("groups", "dp"), None, "mp"),
            P(("groups", "dp")),
            P(("groups", "dp")),
            P(("groups", "dp"), None, None, "mp"),
            P("groups"),
            P("mp"),
            P("mp", "dp", None),
            P("mp", "dp", None),
            P("groups", "mp", "dp"),
        ),
        out_specs=(
            P("groups", "mp"),
            P(("groups", "dp"), None, "mp"),
            P(("groups", "dp"), None, "mp"),
            P("groups", "mp", "dp"),
        ),
        check_vma=False,
    )
```

profile of v0, /device:TPU:0, one launch (start us, length us, event | category | flops | bytes accessed | tf_op | source)
XLA Modules:
  0.0 703.0 jit_solution(7702679912213129711)
XLA Ops:
  7.2 0.0 all-gather.10.cloned.1.call-start
  7.2 0.9 fusion.16
  8.1 0.7 convert_element_type.34
  8.8 0.8 convert_reduce_fusion
  9.5 2.4 fusion.14
  12.0 0.3 fusion.9
  12.2 2.8 pad_maximum_fusion
  15.1 0.0 all-gather.6.cloned.1.call-start
  15.2 0.7 all-gather.6.cloned.1.call-update
  15.9 0.0 all-gather.8.cloned.1.call-start
  15.9 0.6 dynamic-slice
  17.2 0.2 dynamic-update-slice
  17.4 0.0 reduce-scatter.3.cloned.1.call-start
  17.5 48.1 %all-reduce = f32[16]{0:T(128)S(1)} all-reduce(f32[16]{0:T(128)S(1)} %dynamic-update-slice), channel_id=2, replica_groups=mesh['groups'=2,'dp'=8,'mp'=2] {'dp'}, use_global_device_ids=true, to_apply=%add | all-reduce | flops 16 | bytes 128
  65.6 0.1 slice.26
  65.7 0.1 reshape.155
  66.4 353.8 %all-gather.10.cloned.1.call-done = f32[640,2,4096]{2,1,0:T(2,128)} async-done(((f32[80,2,4096]{2,1,0:T(2,128)}), f32[640,2,4096]{2,1,0:T(2,128)}) %all-gather.10.cloned.1.call-update) | async-done | bytes 20971536 | tf_op jit(solution)/shard_map/all_gather | solution.py:9
  420.3 13.6 %slice.29 = f32[560,2,4096]{2,1,0:T(2,128)} slice(f32[640,2,4096]{2,1,0:T(2,128)} %all-gather.10.cloned.1.call-done), slice={[80:640], [0:2], [0:4096]} | slice | bytes 36700160 | tf_op jit(solution)/shard_map/slice | solution.py:11
  433.9 1.7 slice-done
  435.6 32.7 %while.12 = (s32[]{:T(128)}, f32[2]{0:T(128)S(1)}, f32[80,2,4096]{2,1,0:T(2,128)S(1)}, f32[7,2]{1,0:T(8,128)S(1)}, f32[7,80,2,4096]{3,2,1,0:T(2,128)}, /*index=5*/s32[]{:T(128)}) while((s32[]{:T(128)}, f32[2]{0:T(128)S(1)}, f32[80,2,4096]{2,1,0:T(2,128)S(1)}, f32[7,2]{1,0:T(8,128)S(1)}, f32[7,80,2,4096]{3,2,1,0:T(2,128)}, ...), condition=%wide.region_2.3_spmd, body=%wide.region_1.2_spmd.sunk | while | flops 2621444 | bytes 7864469 | solution.py:12
  435.6 4.6 fusion.27
  440.3 4.6 fusion.27
  445.0 4.6 fusion.27
  449.6 4.6 fusion.27
  454.3 4.6 fusion.27
  459.0 4.6 fusion.27
  463.7 4.6 fusion.27
  468.3 1.5 copy.19
  469.8 1.5 copy-done.1
  471.3 0.2 multiply_reduce_fusion.1
  471.6 2.6 psum.28
  474.2 2.3 broadcast_multiply_fusion
  476.4 1.0 copy-done.4
  477.5 2.6 convolution_reduce_fusion
  480.1 2.7 psum.29
  482.7 1.2 multiply_reduce_fusion
  483.9 5.7 fusion.3
  489.6 2.5 all-reduce.1
  492.1 3.4 multiply_convert_fusion
  495.5 51.9 %all-gather.6.cloned.1.call-done = bf16[1,4096,1024]{2,1,0:T(8,128)(2,1)} async-done(((bf16[1,512,1024]{2,1,0:T(8,128)(2,1)}), bf16[1,4096,1024]{2,1,0:T(8,128)(2,1)}) %all-gather.6.cloned.1.call-update) | async-done | bytes 8388624 | tf_op jit(solution)/shard_map/all_gather | solution.py:63
  547.4 9.0 %fusion.7 = f32[384,1024]{1,0:T(8,128)} fusion(bf16[384,4096]{1,0:T(8,128)(2,1)} %bitcast.63, bf16[1,4096,1024]{2,1,0:T(8,128)(2,1)} %all-gather.6.cloned.1.call-done), kind=kOutput, calls=%fused_computation.10 | convolution fusion | flops 3221225472 | bytes 13107200 | tf_op jit(solution)/shard_map/dot_general | solution.py:61
  556.4 0.0 reduce-scatter.5.cloned.1.call-start
  556.5 116.2 %all-gather.8.cloned.1.call-done = bf16[1,4096,1024]{2,1,0:T(8,128)(2,1)} async-done(((bf16[1,512,1024]{2,1,0:T(8,128)(2,1)}), bf16[1,4096,1024]{2,1,0:T(8,128)(2,1)}) %all-gather.8.cloned.1.call-update) | async-done | bytes 8388624 | tf_op jit(solution)/shard_map/all_gather | solution.py:68
  672.7 6.9 fusion.5
  679.6 7.9 %subtract_convert_fusion = bf16[1,4096,1024]{2,1,0:T(8,128)(2,1)} fusion(bf16[1,4096,1024]{2,1,0:T(8,128)(2,1)} %param.19, f32[1024]{0:T(1024)S(1)} %get-tuple-element.43, f32[4096]{0:T(1024)S(1)} %bitcast.68), kind=kLoop, calls=%fused_computation.5 | loop fusion | flops 16777216 | bytes 16797696 | tf_op jit(solution)/shard_map/convert_element_type | solution.py:79
  687.5 1.9 convert_element_type.38
  689.5 5.1 reduce-scatter.5.cloned.1.call-done
  694.5 1.9 convert_element_type.39
  (38 shorter events, 0.2 us)
Async XLA Ops:
  7.2 4.8 copy-start.6
  7.2 5.1 copy-start.3
  7.2 413.1 %all-gather.10.cloned.1.call-start = ((), (), s32[]{:S(2)}) async-start(), calls=%async_computation.6 | async-start | bytes 23592960 | tf_op jit(solution)/shard_map/all_gather | solution.py:9
  15.1 0.8 copy-start.7
  15.1 532.3 %all-gather.6.cloned.1.call-start = ((), (), s32[]{:S(2)}) async-start(), calls=%async_computation.2 | async-start | bytes 9437184 | tf_op jit(solution)/shard_map/all_gather | solution.py:63
  15.9 656.8 %all-gather.8.cloned.1.call-start = ((), (), s32[]{:S(2)}) async-start(), calls=%async_computation.4 | async-start | bytes 9437184 | tf_op jit(solution)/shard_map/all_gather | solution.py:68
  17.4 670.1 %reduce-scatter.3.cloned.1.call-start = ((), (), s32[]{:S(2)}) async-start(), calls=%async_computation.3 | async-start | bytes 2359296 | tf_op jit(solution)/shard_map/reduce_scatter | solution.py:72
  433.9 1.7 slice-start
  469.8 1.5 copy-start.1
  471.3 6.2 copy-start
  476.4 1.1 copy-start.4
  483.9 8.2 %copy-start.5 = (f32[4096]{0:T(1024)S(1)}, f32[4096]{0:T(1024)}, u32[]{:S(2)}) copy-start(f32[4096]{0:T(1024)} %param.16) | copy-start | bytes 49156
  547.4 125.3 %copy-start.2 = (bf16[3,128,4096]{2,1,0:T(8,128)(2,1)S(1)}, bf16[3,128,4096]{2,1,0:T(8,128)(2,1)}, u32[]{:S(2)}) copy-start(bf16[3,128,4096]{2,1,0:T(8,128)(2,1)} %multiply_convert_fusion) | copy-start | bytes 9437188
  556.4 138.1 %reduce-scatter.5.cloned.1.call-start = ((), (), s32[]{:S(2)}) async-start(), calls=%async_computation.5 | async-start | bytes 2359296 | tf_op jit(solution)/shard_map/reduce_scatter | solution.py:73
Sparse Core Ops, SparseCore 0:
  15.2 405.0 all-gather.9
  422.4 124.9 all-gather.5
  549.5 123.1 all-gather.7
  674.8 7.2 reduce-scatter.2
  684.2 10.2 reduce-scatter.4
where the time goes:
time: 704 us; the launch traced here: 703 us
  waiting for transfers between devices  528 us (75%)
  other arithmetic  56.4 us (8%)
  blocking collectives  55.9 us (8%)
  matrix products  26.9 us (4%)
  local copies, waits for them, and re-layouts  20.4 us (3%)
  between operations  15.2 us (2%)
    all_gather x1, waiting for transfers between devices, joined(): pieces = jax.tree.map(lambda part: lax.all_gather(part, axis), value)  354 us
    all_gather x1, waiting for transfers between devices, shards(): lax.all_gather(value_weight, 'dp', axis=1, tiled=True)[0]  116 us
    all_gather x1, waiting for transfers between devices, shards(): lax.all_gather(key_weight, 'dp', axis=1, tiled=True)[0]  51.9 us
    unnamed x1, blocking collectives  48.1 us
    div x7, other arithmetic, combine(): return (joint_count, blended / joint_count[None, :, None])  32.4 us
  transfers between devices with their start and end apart: 5, of which 4 were waited for; matrix products, arithmetic and copies ran while one was open for 13% of the time, Pallas kernels for 0%

commit v1 on v0

--- a/solution.py
+++ b/solution.py
@@ -3,6 +3,27 @@
 import jax.numpy as jnp
 from jax import lax
 from jax.sharding import PartitionSpec as P
+
+
+def collect(x, axis, dim):
+    size, index, extent = (lax.axis_size(axis), lax.axis_index(axis), x.shape[dim])
+    upward = [(i, (i + 1) % size) for i in range(size)]
+    behind = [(i, (i - 1) % size) for i in range(size)]
+    out = jnp.zeros((*x.shape[:dim], size * extent, *x.shape[dim + 1 :]), x.dtype)
+    out = lax.dynamic_update_slice_in_dim(out, x, index * extent, axis=dim)
+    from_left = from_right = x
+    halfway = size // 2
+    for hop in range(1, halfway + 1):
+        from_left = lax.ppermute(from_left, axis, upward)
+        out = lax.dynamic_update_slice_in_dim(
+            out, from_left, (index - hop) % size * extent, axis=dim
+        )
+        if hop < size - halfway:
+            from_right = lax.ppermute(from_right, axis, behind)
+            out = lax.dynamic_update_slice_in_dim(
+                out, from_right, (index + hop) % size * extent, axis=dim
+            )
+    return out
 
 
 def joined(value, axis, join):
@@ -58,11 +79,7 @@
     normed = (ablated * lax.rsqrt(mean_square + 1e-05)[:, None] * norm_gain[None, :]).astype(
         jnp.bfloat16
     )
-    key_sum = jnp.dot(
-        normed,
-        lax.all_gather(key_weight, "dp", axis=1, tiled=True)[0],
-        preferred_element_type=jnp.float32,
-    )
+    key_sum = jnp.dot(normed, collect(key_weight, "dp", 1)[0], preferred_element_type=jnp.float32)
     value_sum = jnp.dot(
         normed,
         lax.all_gather(value_weight, "dp", axis=1, tiled=True)[0],

time: 704 us -> 734 us (1.043)
  waiting for transfers between devices: 528 us -> 455 us
  blocking collectives: 55.9 us -> 113 us
  starting transfers between devices: 0.2 us -> 27.4 us
  local copies, waits for them, and re-layouts: 20.4 us -> 34.2 us
    ppermute x0 -> x7, waiting for transfers between devices: none -> 226 us  [the longest x3 120 us: collect(): from_right = lax.ppermute(from_right, axis, behind)]
    all_gather x1, waiting for transfers between devices: 354 us -> 181 us  [joined(): pieces = jax.tree.map(lambda part: lax.all_gather(part, axis), value)]
    all_gather x1, waiting for transfers between devices: 116 us -> 45.1 us  [shards(): lax.all_gather(value_weight, 'dp', axis=1, tiled=True)[0]]
    unnamed x1, blocking collectives: 48.1 us -> 106 us
    all_gather x1 -> x0, waiting for transfers between devices: 51.9 us -> none  [shards(): lax.all_gather(key_weight, 'dp', axis=1, tiled=True)[0]]
    ppermute x0 -> x7, starting transfers between devices: none -> 27.2 us  [the longest x3 19 us: collect(): from_right = lax.ppermute(from_right, axis, behind)]
    dynamic_update_slice x0 -> x8, local copies, waits for them, and re-layouts: none -> 10.8 us  [the longest x4 5.38 us: collect(): lax.dynamic_update_slice_in_dim(out, from_left, (index - hop) % size * ex...]
  transfers between devices with their start and end apart: 5 -> 11, of which waited for: 4 -> 6; matrix products, arithmetic and copies ran while one was open for 13% -> 14% of each run, Pallas kernels for 0% -> 0%
where the time goes in v1:
time: 734 us; the launch traced here: 733 us
  waiting for transfers between devices  455 us (62%)
  blocking collectives  113 us (15%)
  other arithmetic  59.4 us (8%)
  local copies, waits for them, and re-layouts  34.2 us (5%)
  matrix products  28.5 us (4%)
  starting transfers between devices  27.4 us (4%)
  between operations  15.4 us (2%)
    all_gather x1, waiting for transfers between devices, joined(): pieces = jax.tree.map(lambda part: lax.all_gather(part, axis), value)  181 us
    ppermute x3, waiting for transfers between devices, collect(): from_right = lax.ppermute(from_right, axis, behind)  120 us
    unnamed x1, blocking collectives  106 us
    ppermute x4, waiting for transfers between devices, collect(): from_left = lax.ppermute(from_left, axis, upward)  105 us
    all_gather x1, waiting for transfers between devices, shards(): lax.all_gather(value_weight, 'dp', axis=1, tiled=True)[0]  45.1 us
    div x7, other arithmetic, combine(): return (joint_count, blended / joint_count[None, :, None])  32.4 us
    ppermute x3, starting transfers between devices, collect(): from_right = lax.ppermute(from_right, axis, behind)  19 us
  transfers between devices with their start and end apart: 11, of which 6 were waited for; matrix products, arithmetic and copies ran while one was open for 14% of the time, Pallas kernels for 0%

profile of v1, /device:TPU:0, one launch (start us, length us, event | category | flops | bytes accessed | tf_op | source)
XLA Modules:
  0.0 733.1 jit_solution(14823888851950455569)
XLA Ops:
  9.5 2.4 fusion.17
  12.8 5.7 pad_maximum_fusion
  18.6 3.0 collective-permute-start
  21.6 3.1 collective-permute-start.1
  24.8 105.4 %collective-permute-done = bf16[1,512,1024]{2,1,0:T(8,128)(2,1)S(1)} collective-permute-done((bf16[1,512,1024]{2,1,0:T(8,128)(2,1)S(1)}, bf16[1,512,1024]{2,1,0:T(8,128)(2,1)S(1)}, u32[]{:S(2)}, u32[]{:S(2)}) %collective-permute-start) | collective-permute-done | bytes 1048608 | tf_op jit(solution)/shard_map/ppermute | solution.py:17
  130.1 2.5 collective-permute-start.2
  132.6 37.6 %collective-permute-done.1 = bf16[1,512,1024]{2,1,0:T(8,128)(2,1)} collective-permute-done((bf16[1,512,1024]{2,1,0:T(8,128)(2,1)S(1)}, bf16[1,512,1024]{2,1,0:T(8,128)(2,1)}, u32[]{:S(2)}, u32[]{:S(2)}) %collective-permute-start.1) | collective-permute-done | bytes 1048608 | tf_op jit(solution)/shard_map/ppermute | solution.py:22
  170.2 15.9 %collective-permute-start.3 = (bf16[1,512,1024]{2,1,0:T(8,128)(2,1)}, bf16[1,512,1024]{2,1,0:T(8,128)(2,1)S(1)}, u32[]{:S(2)}, u32[]{:S(2)}) collective-permute-start(bf16[1,512,1024]{2,1,0:T(8,128)(2,1)} %collective-permute-done.1), channel_id=1, source_target_pairs={{0,14},{2,0},{4,2},{6,4},{8,6},{10,8},{12,10},{14,12},{1,15},{3,1}... | collective-permute-start | bytes 3145736 | tf_op jit(solution)/shard_map/ppermute | solution.py:22
  188.4 105.7 %all-reduce = f32[16]{0:T(128)S(1)} all-reduce(f32[16]{0:T(128)S(1)} %dynamic-update-slice), channel_id=2, replica_groups=mesh['groups'=2,'dp'=8,'mp'=2] {'dp'}, use_global_device_ids=true, to_apply=%add | all-reduce | flops 16 | bytes 128
  295.0 4.5 squeeze.50
  299.5 1.0 bitcast_dynamic-update-slice_fusion.7
  300.5 1.0 bitcast_dynamic-update-slice_fusion.6
  301.6 2.3 bitcast_dynamic-update-slice_fusion.5
  303.8 2.0 collective-permute-start.6
  305.9 2.3 bitcast_dynamic-update-slice_fusion.4
  308.1 1.0 bitcast_dynamic-update-slice_fusion.3
  309.2 1.0 bitcast_dynamic-update-slice_fusion.2
  310.2 82.7 %collective-permute-done.5 = bf16[1,512,1024]{2,1,0:T(8,128)(2,1)S(1)} collective-permute-done((bf16[1,512,1024]{2,1,0:T(8,128)(2,1)S(1)}, bf16[1,512,1024]{2,1,0:T(8,128)(2,1)S(1)}, u32[]{:S(2)}, u32[]{:S(2)}) %collective-permute-start.5) | collective-permute-done | bytes 1048608 | tf_op jit(solution)/shard_map/ppermute | solution.py:22
  392.9 1.0 bitcast_dynamic-update-slice_fusion.1
  393.9 1.0 bitcast_dynamic-update-slice_fusion
  394.9 180.6 %all-gather.7.cloned.1.call-done = f32[640,2,4096]{2,1,0:T(2,128)} async-done(((f32[80,2,4096]{2,1,0:T(2,128)}), f32[640,2,4096]{2,1,0:T(2,128)}) %all-gather.7.cloned.1.call-update) | async-done | bytes 20971536 | tf_op jit(solution)/shard_map/all_gather | solution.py:30
  575.5 13.8 %slice.29 = f32[560,2,4096]{2,1,0:T(2,128)} slice(f32[640,2,4096]{2,1,0:T(2,128)} %all-gather.7.cloned.1.call-done), slice={[80:640], [0:2], [0:4096]} | slice | bytes 36700160 | tf_op jit(solution)/shard_map/slice | solution.py:32
  589.4 32.7 %while.12 = (s32[]{:T(128)}, f32[2]{0:T(128)S(1)}, f32[80,2,4096]{2,1,0:T(2,128)S(1)}, f32[7,2]{1,0:T(8,128)S(1)}, f32[7,80,2,4096]{3,2,1,0:T(2,128)}, /*index=5*/s32[]{:T(128)}) while((s32[]{:T(128)}, f32[2]{0:T(128)S(1)}, f32[80,2,4096]{2,1,0:T(2,128)S(1)}, f32[7,2]{1,0:T(8,128)S(1)}, f32[7,80,2,4096]{3,2,1,0:T(2,128)}, ...), condition=%wide.region_2.3_spmd, body=%wide.region_1.2_spmd.sunk | while | flops 2621444 | bytes 7864477 | solution.py:33
  589.4 4.6 fusion.31
  594.1 4.6 fusion.31
  598.8 4.6 fusion.31
  603.4 4.6 fusion.31
  608.1 4.6 fusion.31
  612.8 4.6 fusion.31
  617.4 4.6 fusion.31
  622.1 1.5 copy.19
  623.6 1.5 copy-done.1
  625.4 2.6 psum.28
  628.0 2.5 broadcast_multiply_fusion
  630.5 1.0 copy-done.2
  631.5 2.6 convolution_reduce_fusion
  634.1 2.7 psum.29
  636.7 1.2 multiply_reduce_fusion
  637.9 5.7 fusion.3
  643.6 2.5 all-reduce.1
  646.1 8.0 %fusion.8 = f32[384,1024]{1,0:T(8,128)} fusion(bf16[4096,1024]{1,0:T(8,128)(2,1)} %bitcast_dynamic-update-slice_fusion, bf16[384,4096]{1,0:T(8,128)(2,1)S(1)} %bitcast.76, f32[4096]{0:T(1024)S(1)} %copy-done.6, f32[384]{0:T(512)S(1)} %get-tuple-element.47, f32[4096]{0:T(1024)S(1)} %bitcast.80, f32[384]{0:T(512)S(1)} %psum.29), kind=kOutput, calls=%fused_computation.16 | convolution fusion | flops 3230662656 | bytes 13143040 | tf_op jit(solution)/shard_map/dot_general | solution.py:82
  654.2 3.4 multiply_convert_fusion
  657.6 45.1 %all-gather.5.cloned.1.call-done = bf16[1,4096,1024]{2,1,0:T(8,128)(2,1)} async-done(((bf16[1,512,1024]{2,1,0:T(8,128)(2,1)}), bf16[1,4096,1024]{2,1,0:T(8,128)(2,1)}) %all-gather.5.cloned.1.call-update) | async-done | bytes 8388624 | tf_op jit(solution)/shard_map/all_gather | solution.py:85
  702.7 8.9 %fusion.5 = f32[384,1024]{1,0:T(8,128)} fusion(bf16[384,4096]{1,0:T(8,128)(2,1)} %bitcast.77, bf16[1,4096,1024]{2,1,0:T(8,128)(2,1)} %all-gather.5.cloned.1.call-done), kind=kOutput, calls=%fused_computation.8 | convolution fusion | flops 3221225472 | bytes 13107200 | tf_op jit(solution)/shard_map/dot_general | solution.py:83
  711.6 7.9 %subtract_convert_fusion = bf16[1,4096,1024]{2,1,0:T(8,128)(2,1)} fusion(bf16[1,4096,1024]{2,1,0:T(8,128)(2,1)} %param.19, f32[1024]{0:T(1024)S(1)} %get-tuple-element.43, f32[4096]{0:T(1024)S(1)} %bitcast.82), kind=kLoop, calls=%fused_computation.5 | loop fusion | flops 16777216 | bytes 16797696 | tf_op jit(solution)/shard_map/convert_element_type | solution.py:96
  719.5 1.9 convert_element_type.40
  721.4 3.3 reduce-scatter.5.cloned.1.call-done
  724.7 1.9 convert_element_type.43
  (58 shorter events, 5.5 us)
Async XLA Ops:
  7.2 179.6 %copy-start.7 = (u32[32]{0:T(128)S(1)}, u32[32]{0:T(128)}, u32[]{:S(2)}) copy-start(u32[32]{0:T(128)} %constant.111) | copy-start | bytes 388
  7.2 11.4 %copy-start.3 = (bf16[1,512,1024]{2,1,0:T(8,128)(2,1)S(1)}, bf16[1,512,1024]{2,1,0:T(8,128)(2,1)}, u32[]{:S(2)}) copy-start(bf16[1,512,1024]{2,1,0:T(8,128)(2,1)} %param.17) | copy-start | bytes 3145732
  7.2 568.3 %all-gather.7.cloned.1.call-start = ((), (), s32[]{:S(2)}) async-start(), calls=%async_computation.5 | async-start | bytes 23592960 | tf_op jit(solution)/shard_map/all_gather | solution.py:30
  18.6 684.1 %all-gather.5.cloned.1.call-start = ((), (), s32[]{:S(2)}) async-start(), calls=%async_computation.3 | async-start | bytes 9437184 | tf_op jit(solution)/shard_map/all_gather | solution.py:85
  18.6 111.5 %collective-permute-start = (bf16[1,512,1024]{2,1,0:T(8,128)(2,1)S(1)}, bf16[1,512,1024]{2,1,0:T(8,128)(2,1)S(1)}, u32[]{:S(2)}, u32[]{:S(2)}) collective-permute-start(bf16[1,512,1024]{2,1,0:T(8,128)(2,1)S(1)} %copy-done.3), channel_id=1, source_target_pairs={{0,2},{2,4},{4,6},{6,8},{8,10},{10,12},{12,14},{14,0},{1,3},{3,5},... | collective-permute-start | bytes 3145736 | tf_op jit(solution)/shard_map/ppermute | solution.py:17
  21.6 148.6 %collective-permute-start.1 = (bf16[1,512,1024]{2,1,0:T(8,128)(2,1)S(1)}, bf16[1,512,1024]{2,1,0:T(8,128)(2,1)}, u32[]{:S(2)}, u32[]{:S(2)}) collective-permute-start(bf16[1,512,1024]{2,1,0:T(8,128)(2,1)S(1)} %copy-done.3), channel_id=1, source_target_pairs={{0,14},{2,0},{4,2},{6,4},{8,6},{10,8},{12,10},{14,12},{1,15},{3,1}... | collective-permute-start | bytes 3145736 | tf_op jit(solution)/shard_map/ppermute | solution.py:22
  130.1 56.0 %copy-start.4 = (bf16[1,512,1024]{2,1,0:T(8,128)(2,1)}, bf16[1,512,1024]{2,1,0:T(8,128)(2,1)S(1)}, u32[]{:S(2)}) copy-start(bf16[1,512,1024]{2,1,0:T(8,128)(2,1)S(1)} %collective-permute-done) | copy-start | bytes 3145732
  130.1 56.0 %collective-permute-start.2 = (bf16[1,512,1024]{2,1,0:T(8,128)(2,1)S(1)}, bf16[1,512,1024]{2,1,0:T(8,128)(2,1)}, u32[]{:S(2)}, u32[]{:S(2)}) collective-permute-start(bf16[1,512,1024]{2,1,0:T(8,128)(2,1)S(1)} %collective-permute-done), channel_id=1, source_target_pairs={{0,2},{2,4},{4,6},{6,8},{8,10},{10,12},{12,14},{14,0},{1,3},{3,5},... | collective-permute-start | bytes 3145736 | tf_op jit(solution)/shard_map/ppermute | solution.py:17
  170.2 131.3 %collective-permute-start.3 = (bf16[1,512,1024]{2,1,0:T(8,128)(2,1)}, bf16[1,512,1024]{2,1,0:T(8,128)(2,1)S(1)}, u32[]{:S(2)}, u32[]{:S(2)}) collective-permute-start(bf16[1,512,1024]{2,1,0:T(8,128)(2,1)} %collective-permute-done.1), channel_id=1, source_target_pairs={{0,14},{2,0},{4,2},{6,4},{8,6},{10,8},{12,10},{14,12},{1,15},{3,1}... | collective-permute-start | bytes 3145736 | tf_op jit(solution)/shard_map/ppermute | solution.py:22
  186.1 117.7 %collective-permute-start.4 = (bf16[1,512,1024]{2,1,0:T(8,128)(2,1)}, bf16[1,512,1024]{2,1,0:T(8,128)(2,1)S(1)}, u32[]{:S(2)}, u32[]{:S(2)}) collective-permute-start(bf16[1,512,1024]{2,1,0:T(8,128)(2,1)} %collective-permute-done.2), channel_id=1, source_target_pairs={{0,2},{2,4},{4,6},{6,8},{8,10},{10,12},{12,14},{14,0},{1,3},{3,5},... | collective-permute-start | bytes 3145736 | tf_op jit(solution)/shard_map/ppermute | solution.py:17
  188.3 531.2 %reduce-scatter.3.cloned.1.call-start = ((), (), s32[]{:S(2)}) async-start(), calls=%async_computation.2 | async-start | bytes 2359296 | tf_op jit(solution)/shard_map/reduce_scatter | solution.py:89
  295.0 5.5 copy-start.5
  301.6 91.3 %collective-permute-start.5 = (bf16[1,512,1024]{2,1,0:T(8,128)(2,1)S(1)}, bf16[1,512,1024]{2,1,0:T(8,128)(2,1)S(1)}, u32[]{:S(2)}, u32[]{:S(2)}) collective-permute-start(bf16[1,512,1024]{2,1,0:T(8,128)(2,1)S(1)} %collective-permute-done.3), channel_id=1, source_target_pairs={{0,14},{2,0},{4,2},{6,4},{8,6},{10,8},{12,10},{14,12},{1,15},{3,1}... | collective-permute-start | bytes 3145736 | tf_op jit(solution)/shard_map/ppermute | solution.py:22
  303.8 90.1 %collective-permute-start.6 = (bf16[1,512,1024]{2,1,0:T(8,128)(2,1)S(1)}, bf16[1,512,1024]{2,1,0:T(8,128)(2,1)S(1)}, u32[]{:S(2)}, u32[]{:S(2)}) collective-permute-start(bf16[1,512,1024]{2,1,0:T(8,128)(2,1)S(1)} %collective-permute-done.4), channel_id=1, source_target_pairs={{0,2},{2,4},{4,6},{6,8},{8,10},{10,12},{12,14},{14,0},{1,3},{3,5},... | collective-permute-start | bytes 3145736 | tf_op jit(solution)/shard_map/ppermute | solution.py:17
  575.5 13.9 %slice-start = ((f32[640,2,4096]{2,1,0:T(2,128)}), f32[80,2,4096]{2,1,0:T(2,128)S(1)}, s32[]{:S(2)}) async-start(f32[640,2,4096]{2,1,0:T(2,128)} %all-gather.7.cloned.1.call-done), calls=%async_computation.6 | async-start | bytes 5242880 | tf_op jit(solution)/shard_map/slice | solution.py:31
  623.6 1.5 copy-start.1
  625.1 6.4 copy-start
  630.4 1.1 copy-start.2
  637.9 8.2 %copy-start.6 = (f32[4096]{0:T(1024)S(1)}, f32[4096]{0:T(1024)}, u32[]{:S(2)}) copy-start(f32[4096]{0:T(1024)} %param.16) | copy-start | bytes 49156
  654.2 70.5 %reduce-scatter.5.cloned.1.call-start = ((), (), s32[]{:S(2)}) async-start(), calls=%async_computation.4 | async-start | bytes 2359296 | tf_op jit(solution)/shard_map/reduce_scatter | solution.py:90
Sparse Core Ops, SparseCore 0:
  18.7 556.7 all-gather.6
  577.7 124.9 all-gather.4
  704.9 7.2 reduce-scatter.2
  714.4 10.2 reduce-scatter.4
